TPU v7x, 512 devices: a whole 4x4x16 slice. The times are simulated.
512 devices in a mesh: prow: 16 (over y, x), pcol: 32 (over z, core).
Axes of the slice: x: 4, y: 4, z: 16, core: 2. Of those that a mesh axis runs over, the one named last changes fastest.
Arguments:
- factor_tiles: bfloat16 [16, 1024, 1, 16, 1024], P(None, 'pcol', None, 'prow'), may hold values from -0.03125 to 0.03125
- inverse_blocks: bfloat16 [1, 16, 1024, 1024], P(None, 'prow'), may hold values from -1 to 3, as said below
- demand: bfloat16 [16, 1024, 256], P(None, 'pcol'), may hold values from -6 to 6
Outputs:
- solved: bfloat16 [1, 16, 1024, 256], P(None, 'prow')
Inputs may be any that keep to these rules, and one draw needn't show every extreme that they name: `inverse_blocks`: each [1024, 1024] block is lower triangular with a positive diagonal.
All inputs are finite; a program needn't handle non-finite values.
Results may differ from a plain program's by a relative error of at most 0.0075.
Values may be sent and summed in bfloat16 or wider, within the bound.
A program may use at most 64 MiB of HBM per device.

v0:
```python
import jax
import jax.numpy as jnp
from jax import lax
from jax.sharding import PartitionSpec as P


def on_device(factor_tiles, inverse_blocks, demand):
    block_count, slice_rows, col_slots, single, block_width = factor_tiles.shape
    columns = demand.shape[2]
    prow_size = lax.axis_size("prow")
    my_row = lax.axis_index("prow")
    row_tiles = factor_tiles.reshape(block_count, slice_rows, col_slots * block_width)
    inverse = inverse_blocks.reshape(col_slots, block_width, block_width)
    owned_blocks = jnp.zeros((col_slots, block_width, columns), jnp.bfloat16)
    pending = jnp.zeros((block_count, slice_rows, columns), jnp.float32)

    def advance(step_index, carried):
        owned_blocks, pending = carried
        owner_row = step_index % prow_size
        slot_index = step_index // prow_size
        is_owner = my_row == owner_row
        partial_sum = lax.dynamic_index_in_dim(pending, step_index, 0, keepdims=False)
        summed = lax.psum(partial_sum, "prow")
        target = lax.dynamic_index_in_dim(demand, step_index, 0, keepdims=False)
        residual = (target.astype(jnp.float32) - summed).astype(jnp.bfloat16)
        block_inv = lax.dynamic_index_in_dim(inverse, slot_index, 0, keepdims=False)
        apply_running = jnp.zeros((block_width, columns), jnp.float32)
        segment = lax.all_gather(residual, "pcol", axis=0, tiled=True)
        solved = lax.cond(
            is_owner,
            lambda: jnp.dot(block_inv, segment, preferred_element_type=jnp.float32),
            lambda: apply_running,
        ).astype(jnp.bfloat16)
        owned_blocks = jnp.where(
            is_owner,
            lax.dynamic_update_index_in_dim(owned_blocks, solved, slot_index, 0),
            owned_blocks,
        )
        pending = lax.cond(
            is_owner,
            lambda running: running
            + jnp.einsum("krw,wn->krn", row_tiles, solved, preferred_element_type=jnp.float32),
            lambda running: running,
            pending,
        )
        return (owned_blocks, pending)

    owned_blocks, pending = lax.fori_loop(0, block_count, advance, (owned_blocks, pending))
    return owned_blocks.reshape(col_slots, 1, block_width, columns)


def solution(mesh):
    placed = (
        P(None, "pcol", None, "prow", None),
        P(None, "prow", None, None),
        P(None, "pcol", None),
    )
    return jax.shard_map(
        on_device,
        mesh=mesh,
        in_specs=placed,
        out_specs=P(None, "prow", None, None),
        check_vma=False,
    )
```

profile of v0, /device:TPU:1, one launch (start us, length us, event | category | flops | bytes accessed | tf_op | source)
XLA Modules:
  0.0 1639.2 jit_solution(5200162110590774931)
XLA Ops:
  0.1 1638.4 %while.21 = (s32[]{:T(128)}, bf16[1,1024,256]{2,1,0:T(8,128)(2,1)S(1)}, f32[16,32,256]{2,1,0:T(8,128)S(1)}, s32[]{:T(128)}, bf16[16,32,256]{2,1,0:T(8,128)(2,1)}...) while((s32[]{:T(128)}, ...), condition=%wide.region_6.7_spmd.clone, body=%wide.region_0.6_spmd.clone.sunk | while | flops 806256640 | bytes 13320484 | solution.py:48
  0.1 61.6 %psum.16 = f32[32,256]{1,0:T(8,128)S(1)} all-reduce(f32[32,256]{1,0:T(8,128)S(1)} %dynamic-slice_bitcast_fusion.2), channel_id=1, replica_groups=mesh['prow'=16,'pcol'=32] {'prow'}, use_global_device_ids=true, to_apply=%region_1.1 | all-reduce | flops 8192 | bytes 65536 | tf_op jit(solution)/shard_map/while/body/eval_jaxpr/psum | solution.py:23
  62.4 52.0 %all_gather.12 = bf16[1024,256]{1,0:T(8,128)(2,1)S(1)} all-gather(bf16[32,256]{1,0:T(8,128)(2,1)S(1)} %fusion.10), channel_id=1, replica_groups=mesh['prow'=16,'pcol'=32] {'pcol'}, dimensions={0}, use_global_device_ids=true | all-gather | bytes 540672 | tf_op jit(solution)/shard_map/while/body/eval_jaxpr/all_gather | solution.py:28
  114.4 4.2 conditional.6
  114.4 3.2 fusion.2
  117.6 1.0 copy.7
  118.6 1.5 conditional.7
  118.6 1.5 convolution_add_fusion
  120.4 55.8 %psum.16 = f32[32,256]{1,0:T(8,128)S(1)} all-reduce(f32[32,256]{1,0:T(8,128)S(1)} %dynamic-slice_bitcast_fusion.2), channel_id=1, replica_groups=mesh['prow'=16,'pcol'=32] {'prow'}, use_global_device_ids=true, to_apply=%region_1.1 | all-reduce | flops 8192 | bytes 65536 | tf_op jit(solution)/shard_map/while/body/eval_jaxpr/psum | solution.py:23
  176.9 42.0 %all_gather.12 = bf16[1024,256]{1,0:T(8,128)(2,1)S(1)} all-gather(bf16[32,256]{1,0:T(8,128)(2,1)S(1)} %fusion.10), channel_id=1, replica_groups=mesh['prow'=16,'pcol'=32] {'pcol'}, dimensions={0}, use_global_device_ids=true | all-gather | bytes 540672 | tf_op jit(solution)/shard_map/while/body/eval_jaxpr/all_gather | solution.py:28
  218.8 0.9 conditional.6
  218.8 0.8 broadcast.8
  220.5 58.3 %psum.16 = f32[32,256]{1,0:T(8,128)S(1)} all-reduce(f32[32,256]{1,0:T(8,128)S(1)} %dynamic-slice_bitcast_fusion.2), channel_id=1, replica_groups=mesh['prow'=16,'pcol'=32] {'prow'}, use_global_device_ids=true, to_apply=%region_1.1 | all-reduce | flops 8192 | bytes 65536 | tf_op jit(solution)/shard_map/while/body/eval_jaxpr/psum | solution.py:23
  279.5 44.1 %all_gather.12 = bf16[1024,256]{1,0:T(8,128)(2,1)S(1)} all-gather(bf16[32,256]{1,0:T(8,128)(2,1)S(1)} %fusion.10), channel_id=1, replica_groups=mesh['prow'=16,'pcol'=32] {'pcol'}, dimensions={0}, use_global_device_ids=true | all-gather | bytes 540672 | tf_op jit(solution)/shard_map/while/body/eval_jaxpr/all_gather | solution.py:28
  323.6 0.9 conditional.6
  323.6 0.8 broadcast.8
  325.3 55.8 %psum.16 = f32[32,256]{1,0:T(8,128)S(1)} all-reduce(f32[32,256]{1,0:T(8,128)S(1)} %dynamic-slice_bitcast_fusion.2), channel_id=1, replica_groups=mesh['prow'=16,'pcol'=32] {'prow'}, use_global_device_ids=true, to_apply=%region_1.1 | all-reduce | flops 8192 | bytes 65536 | tf_op jit(solution)/shard_map/while/body/eval_jaxpr/psum | solution.py:23
  381.8 42.0 %all_gather.12 = bf16[1024,256]{1,0:T(8,128)(2,1)S(1)} all-gather(bf16[32,256]{1,0:T(8,128)(2,1)S(1)} %fusion.10), channel_id=1, replica_groups=mesh['prow'=16,'pcol'=32] {'pcol'}, dimensions={0}, use_global_device_ids=true | all-gather | bytes 540672 | tf_op jit(solution)/shard_map/while/body/eval_jaxpr/all_gather | solution.py:28
  423.8 0.9 conditional.6
  423.8 0.8 broadcast.8
  425.4 55.8 %psum.16 = f32[32,256]{1,0:T(8,128)S(1)} all-reduce(f32[32,256]{1,0:T(8,128)S(1)} %dynamic-slice_bitcast_fusion.2), channel_id=1, replica_groups=mesh['prow'=16,'pcol'=32] {'prow'}, use_global_device_ids=true, to_apply=%region_1.1 | all-reduce | flops 8192 | bytes 65536 | tf_op jit(solution)/shard_map/while/body/eval_jaxpr/psum | solution.py:23
  481.9 43.9 %all_gather.12 = bf16[1024,256]{1,0:T(8,128)(2,1)S(1)} all-gather(bf16[32,256]{1,0:T(8,128)(2,1)S(1)} %fusion.10), channel_id=1, replica_groups=mesh['prow'=16,'pcol'=32] {'pcol'}, dimensions={0}, use_global_device_ids=true | all-gather | bytes 540672 | tf_op jit(solution)/shard_map/while/body/eval_jaxpr/all_gather | solution.py:28
  525.8 0.9 conditional.6
  525.8 0.8 broadcast.8
  527.5 55.8 %psum.16 = f32[32,256]{1,0:T(8,128)S(1)} all-reduce(f32[32,256]{1,0:T(8,128)S(1)} %dynamic-slice_bitcast_fusion.2), channel_id=1, replica_groups=mesh['prow'=16,'pcol'=32] {'prow'}, use_global_device_ids=true, to_apply=%region_1.1 | all-reduce | flops 8192 | bytes 65536 | tf_op jit(solution)/shard_map/while/body/eval_jaxpr/psum | solution.py:23
  584.0 42.0 %all_gather.12 = bf16[1024,256]{1,0:T(8,128)(2,1)S(1)} all-gather(bf16[32,256]{1,0:T(8,128)(2,1)S(1)} %fusion.10), channel_id=1, replica_groups=mesh['prow'=16,'pcol'=32] {'pcol'}, dimensions={0}, use_global_device_ids=true | all-gather | bytes 540672 | tf_op jit(solution)/shard_map/while/body/eval_jaxpr/all_gather | solution.py:28
  625.9 0.9 conditional.6
  625.9 0.8 broadcast.8
  627.6 55.8 %psum.16 = f32[32,256]{1,0:T(8,128)S(1)} all-reduce(f32[32,256]{1,0:T(8,128)S(1)} %dynamic-slice_bitcast_fusion.2), channel_id=1, replica_groups=mesh['prow'=16,'pcol'=32] {'prow'}, use_global_device_ids=true, to_apply=%region_1.1 | all-reduce | flops 8192 | bytes 65536 | tf_op jit(solution)/shard_map/while/body/eval_jaxpr/psum | solution.py:23
  684.1 43.9 %all_gather.12 = bf16[1024,256]{1,0:T(8,128)(2,1)S(1)} all-gather(bf16[32,256]{1,0:T(8,128)(2,1)S(1)} %fusion.10), channel_id=1, replica_groups=mesh['prow'=16,'pcol'=32] {'pcol'}, dimensions={0}, use_global_device_ids=true | all-gather | bytes 540672 | tf_op jit(solution)/shard_map/while/body/eval_jaxpr/all_gather | solution.py:28
  728.0 0.9 conditional.6
  728.0 0.8 broadcast.8
  729.7 55.8 %psum.16 = f32[32,256]{1,0:T(8,128)S(1)} all-reduce(f32[32,256]{1,0:T(8,128)S(1)} %dynamic-slice_bitcast_fusion.2), channel_id=1, replica_groups=mesh['prow'=16,'pcol'=32] {'prow'}, use_global_device_ids=true, to_apply=%region_1.1 | all-reduce | flops 8192 | bytes 65536 | tf_op jit(solution)/shard_map/while/body/eval_jaxpr/psum | solution.py:23
  786.1 42.0 %all_gather.12 = bf16[1024,256]{1,0:T(8,128)(2,1)S(1)} all-gather(bf16[32,256]{1,0:T(8,128)(2,1)S(1)} %fusion.10), channel_id=1, replica_groups=mesh['prow'=16,'pcol'=32] {'pcol'}, dimensions={0}, use_global_device_ids=true | all-gather | bytes 540672 | tf_op jit(solution)/shard_map/while/body/eval_jaxpr/all_gather | solution.py:28
  828.1 0.9 conditional.6
  828.1 0.8 broadcast.8
  829.8 55.8 %psum.16 = f32[32,256]{1,0:T(8,128)S(1)} all-reduce(f32[32,256]{1,0:T(8,128)S(1)} %dynamic-slice_bitcast_fusion.2), channel_id=1, replica_groups=mesh['prow'=16,'pcol'=32] {'prow'}, use_global_device_ids=true, to_apply=%region_1.1 | all-reduce | flops 8192 | bytes 65536 | tf_op jit(solution)/shard_map/while/body/eval_jaxpr/psum | solution.py:23
  886.3 43.9 %all_gather.12 = bf16[1024,256]{1,0:T(8,128)(2,1)S(1)} all-gather(bf16[32,256]{1,0:T(8,128)(2,1)S(1)} %fusion.10), channel_id=1, replica_groups=mesh['prow'=16,'pcol'=32] {'pcol'}, dimensions={0}, use_global_device_ids=true | all-gather | bytes 540672 | tf_op jit(solution)/shard_map/while/body/eval_jaxpr/all_gather | solution.py:28
  930.2 0.9 conditional.6
  930.2 0.8 broadcast.8
  931.8 55.8 %psum.16 = f32[32,256]{1,0:T(8,128)S(1)} all-reduce(f32[32,256]{1,0:T(8,128)S(1)} %dynamic-slice_bitcast_fusion.2), channel_id=1, replica_groups=mesh['prow'=16,'pcol'=32] {'prow'}, use_global_device_ids=true, to_apply=%region_1.1 | all-reduce | flops 8192 | bytes 65536 | tf_op jit(solution)/shard_map/while/body/eval_jaxpr/psum | solution.py:23
  988.3 42.0 %all_gather.12 = bf16[1024,256]{1,0:T(8,128)(2,1)S(1)} all-gather(bf16[32,256]{1,0:T(8,128)(2,1)S(1)} %fusion.10), channel_id=1, replica_groups=mesh['prow'=16,'pcol'=32] {'pcol'}, dimensions={0}, use_global_device_ids=true | all-gather | bytes 540672 | tf_op jit(solution)/shard_map/while/body/eval_jaxpr/all_gather | solution.py:28
  1030.3 0.9 conditional.6
  1031.9 55.8 %psum.16 = f32[32,256]{1,0:T(8,128)S(1)} all-reduce(f32[32,256]{1,0:T(8,128)S(1)} %dynamic-slice_bitcast_fusion.2), channel_id=1, replica_groups=mesh['prow'=16,'pcol'=32] {'prow'}, use_global_device_ids=true, to_apply=%region_1.1 | all-reduce | flops 8192 | bytes 65536 | tf_op jit(solution)/shard_map/while/body/eval_jaxpr/psum | solution.py:23
  1088.4 43.9 %all_gather.12 = bf16[1024,256]{1,0:T(8,128)(2,1)S(1)} all-gather(bf16[32,256]{1,0:T(8,128)(2,1)S(1)} %fusion.10), channel_id=1, replica_groups=mesh['prow'=16,'pcol'=32] {'pcol'}, dimensions={0}, use_global_device_ids=true | all-gather | bytes 540672 | tf_op jit(solution)/shard_map/while/body/eval_jaxpr/all_gather | solution.py:28
  1132.3 0.9 conditional.6
  1134.0 55.8 %psum.16 = f32[32,256]{1,0:T(8,128)S(1)} all-reduce(f32[32,256]{1,0:T(8,128)S(1)} %dynamic-slice_bitcast_fusion.2), channel_id=1, replica_groups=mesh['prow'=16,'pcol'=32] {'prow'}, use_global_device_ids=true, to_apply=%region_1.1 | all-reduce | flops 8192 | bytes 65536 | tf_op jit(solution)/shard_map/while/body/eval_jaxpr/psum | solution.py:23
  1190.5 42.0 %all_gather.12 = bf16[1024,256]{1,0:T(8,128)(2,1)S(1)} all-gather(bf16[32,256]{1,0:T(8,128)(2,1)S(1)} %fusion.10), channel_id=1, replica_groups=mesh['prow'=16,'pcol'=32] {'pcol'}, dimensions={0}, use_global_device_ids=true | all-gather | bytes 540672 | tf_op jit(solution)/shard_map/while/body/eval_jaxpr/all_gather | solution.py:28
  1232.5 0.9 conditional.6
  1234.1 55.8 %psum.16 = f32[32,256]{1,0:T(8,128)S(1)} all-reduce(f32[32,256]{1,0:T(8,128)S(1)} %dynamic-slice_bitcast_fusion.2), channel_id=1, replica_groups=mesh['prow'=16,'pcol'=32] {'prow'}, use_global_device_ids=true, to_apply=%region_1.1 | all-reduce | flops 8192 | bytes 65536 | tf_op jit(solution)/shard_map/while/body/eval_jaxpr/psum | solution.py:23
  1290.6 43.9 %all_gather.12 = bf16[1024,256]{1,0:T(8,128)(2,1)S(1)} all-gather(bf16[32,256]{1,0:T(8,128)(2,1)S(1)} %fusion.10), channel_id=1, replica_groups=mesh['prow'=16,'pcol'=32] {'pcol'}, dimensions={0}, use_global_device_ids=true | all-gather | bytes 540672 | tf_op jit(solution)/shard_map/while/body/eval_jaxpr/all_gather | solution.py:28
  1334.5 0.9 conditional.6
  1336.2 55.8 %psum.16 = f32[32,256]{1,0:T(8,128)S(1)} all-reduce(f32[32,256]{1,0:T(8,128)S(1)} %dynamic-slice_bitcast_fusion.2), channel_id=1, replica_groups=mesh['prow'=16,'pcol'=32] {'prow'}, use_global_device_ids=true, to_apply=%region_1.1 | all-reduce | flops 8192 | bytes 65536 | tf_op jit(solution)/shard_map/while/body/eval_jaxpr/psum | solution.py:23
  1392.7 42.0 %all_gather.12 = bf16[1024,256]{1,0:T(8,128)(2,1)S(1)} all-gather(bf16[32,256]{1,0:T(8,128)(2,1)S(1)} %fusion.10), channel_id=1, replica_groups=mesh['prow'=16,'pcol'=32] {'pcol'}, dimensions={0}, use_global_device_ids=true | all-gather | bytes 540672 | tf_op jit(solution)/shard_map/while/body/eval_jaxpr/all_gather | solution.py:28
  1434.6 0.9 conditional.6
  1434.6 0.8 broadcast.8
  1436.3 55.8 %psum.16 = f32[32,256]{1,0:T(8,128)S(1)} all-reduce(f32[32,256]{1,0:T(8,128)S(1)} %dynamic-slice_bitcast_fusion.2), channel_id=1, replica_groups=mesh['prow'=16,'pcol'=32] {'prow'}, use_global_device_ids=true, to_apply=%region_1.1 | all-reduce | flops 8192 | bytes 65536 | tf_op jit(solution)/shard_map/while/body/eval_jaxpr/psum | solution.py:23
  1492.8 43.9 %all_gather.12 = bf16[1024,256]{1,0:T(8,128)(2,1)S(1)} all-gather(bf16[32,256]{1,0:T(8,128)(2,1)S(1)} %fusion.10), channel_id=1, replica_groups=mesh['prow'=16,'pcol'=32] {'pcol'}, dimensions={0}, use_global_device_ids=true | all-gather | bytes 540672 | tf_op jit(solution)/shard_map/while/body/eval_jaxpr/all_gather | solution.py:28
  1536.7 0.9 conditional.6
  1536.7 0.8 broadcast.8
  1538.4 55.8 %psum.16 = f32[32,256]{1,0:T(8,128)S(1)} all-reduce(f32[32,256]{1,0:T(8,128)S(1)} %dynamic-slice_bitcast_fusion.2), channel_id=1, replica_groups=mesh['prow'=16,'pcol'=32] {'prow'}, use_global_device_ids=true, to_apply=%region_1.1 | all-reduce | flops 8192 | bytes 65536 | tf_op jit(solution)/shard_map/while/body/eval_jaxpr/psum | solution.py:23
  1594.8 42.0 %all_gather.12 = bf16[1024,256]{1,0:T(8,128)(2,1)S(1)} all-gather(bf16[32,256]{1,0:T(8,128)(2,1)S(1)} %fusion.10), channel_id=1, replica_groups=mesh['prow'=16,'pcol'=32] {'pcol'}, dimensions={0}, use_global_device_ids=true | all-gather | bytes 540672 | tf_op jit(solution)/shard_map/while/body/eval_jaxpr/all_gather | solution.py:28
  1636.8 0.9 conditional.6
  1636.8 0.8 broadcast.8
  (118 shorter events, 27.7 us)
Async XLA Ops:
  114.4 4.2 copy-start
  218.8 1.4 copy-start
  323.6 1.4 copy-start
  423.8 1.4 copy-start
  525.8 1.4 copy-start
  625.9 1.4 copy-start
  728.0 1.4 copy-start
  828.1 1.4 copy-start
  930.2 1.4 copy-start
  1030.3 1.4 copy-start
  1132.3 1.4 copy-start
  1232.5 1.4 copy-start
  1334.5 1.4 copy-start
  1434.6 1.4 copy-start
  1536.7 1.4 copy-start
  1636.8 1.4 copy-start
  1638.4 0.8 copy-start.1
where the time goes:
time: 1640 us
  blocking collectives  1600 us (98%)
  local copies, waits for them, and re-layouts  23 us (1%)
    psum x16, blocking collectives, advance(): summed = lax.psum(partial_sum, 'prow')  901 us
    all_gather x16, blocking collectives, advance(): segment = lax.all_gather(residual, 'pcol', axis=0, tiled=True)  695 us

commit v1 on v0

--- a/solution.py
+++ b/solution.py
@@ -25,7 +25,9 @@
         residual = (target.astype(jnp.float32) - summed).astype(jnp.bfloat16)
         block_inv = lax.dynamic_index_in_dim(inverse, slot_index, 0, keepdims=False)
         apply_running = jnp.zeros((block_width, columns), jnp.float32)
-        segment = lax.all_gather(residual, "pcol", axis=0, tiled=True)
+        segment = jnp.concatenate(
+            lax.all_to_all(jnp.stack([residual] * lax.axis_size("pcol")), "pcol", 0, 0), axis=0
+        )
         solved = lax.cond(
             is_owner,
             lambda: jnp.dot(block_inv, segment, preferred_element_type=jnp.float32),

time: 1640 us -> 1800 us (1.098)
  blocking collectives: 1600 us -> 899 us
  waiting for transfers between devices: 0 us -> 536 us
  starting transfers between devices: 0 us -> 303 us
    all_gather x16 -> x0, blocking collectives: 695 us -> none  [advance(): segment = lax.all_gather(residual, 'pcol', axis=0, tiled=True)]
    all_to_all x0 -> x16, waiting for transfers between devices: none -> 536 us  [advance(): lax.all_to_all(jnp.stack([residual] * lax.axis_size('pcol')), 'pcol', 0, 0)]
    all_to_all x0 -> x16, starting transfers between devices: none -> 303 us  [advance(): lax.all_to_all(jnp.stack([residual] * lax.axis_size('pcol')), 'pcol', 0, 0)]
  transfers between devices with their start and end apart: 0 -> 16, of which waited for: 0 -> 16; matrix products, arithmetic and copies ran while one was open for 0% -> 0% of each run, Pallas kernels for 0% -> 0%
where the time goes in v1:
time: 1800 us
  blocking collectives  899 us (50%)
  waiting for transfers between devices  536 us (30%)
  starting transfers between devices  303 us (17%)
  local copies, waits for them, and re-layouts  36.7 us (2%)
    psum x16, blocking collectives, advance(): summed = lax.psum(partial_sum, 'prow')  899 us
    all_to_all x16, waiting for transfers between devices, advance(): lax.all_to_all(jnp.stack([residual] * lax.axis_size('pcol')), 'pcol', 0, 0)  536 us
    all_to_all x16, starting transfers between devices, advance(): lax.all_to_all(jnp.stack([residual] * lax.axis_size('pcol')), 'pcol', 0, 0)  303 us
  transfers between devices with their start and end apart: 16, of which 16 were waited for; matrix products, arithmetic and copies ran while one was open for 0% of the time, Pallas kernels for 0%

profile of v1, /device:TPU:1, one launch (start us, length us, event | category | flops | bytes accessed | tf_op | source)
XLA Modules:
  0.0 1795.4 jit_solution(15111454151850758994)
XLA Ops:
  0.1 1794.6 %while.21 = (s32[]{:T(128)}, bf16[1,1024,256]{2,1,0:T(8,128)(2,1)S(1)}, f32[16,32,256]{2,1,0:T(8,128)S(1)}, s32[]{:T(128)}, bf16[16,32,256]{2,1,0:T(8,128)(2,1)}...) while((s32[]{:T(128)}, ...), condition=%wide.region_6.7_spmd.clone, body=%wide.region_0.6_spmd.clone.sunk | while | flops 806256640 | bytes 14893380 | solution.py:50
  0.1 61.6 %psum.16 = f32[32,256]{1,0:T(8,128)S(1)} all-reduce(f32[32,256]{1,0:T(8,128)S(1)} %dynamic-slice_bitcast_fusion.2), channel_id=1, replica_groups=mesh['prow'=16,'pcol'=32] {'prow'}, use_global_device_ids=true, to_apply=%region_1.1 | all-reduce | flops 8192 | bytes 65536 | tf_op jit(solution)/shard_map/while/body/eval_jaxpr/psum | solution.py:23
  63.2 29.8 %all-to-all-start = ((bf16[32,32,256]{2,1,0:T(8,128)(2,1)}), bf16[32,32,256]{2,1,0:T(8,128)(2,1)S(1)}, u32[]{:S(2)}, u32[]{:S(2)}) async-start(bf16[32,32,256]{2,1,0:T(8,128)(2,1)} %stack.8), calls=%async_computation | async-start | bytes 1048576 | tf_op jit(solution)/shard_map/while/body/eval_jaxpr/all_to_all | solution.py:29
  93.0 33.5 %all-to-all-done = bf16[32,32,256]{2,1,0:T(8,128)(2,1)S(1)} async-done(((bf16[32,32,256]{2,1,0:T(8,128)(2,1)}), bf16[32,32,256]{2,1,0:T(8,128)(2,1)S(1)}, u32[]{:S(2)}, u32[]{:S(2)}) %all-to-all-start) | async-done | bytes 524320 | tf_op jit(solution)/shard_map/while/body/eval_jaxpr/all_to_all | solution.py:29
  126.5 4.2 conditional.6
  126.5 3.2 fusion.2
  129.7 1.0 copy.7
  130.8 1.5 conditional.7
  130.8 1.5 convolution_add_fusion
  132.5 56.1 %psum.16 = f32[32,256]{1,0:T(8,128)S(1)} all-reduce(f32[32,256]{1,0:T(8,128)S(1)} %dynamic-slice_bitcast_fusion.2), channel_id=1, replica_groups=mesh['prow'=16,'pcol'=32] {'prow'}, use_global_device_ids=true, to_apply=%region_1.1 | all-reduce | flops 8192 | bytes 65536 | tf_op jit(solution)/shard_map/while/body/eval_jaxpr/psum | solution.py:23
  190.2 17.5 all-to-all-start
  207.7 33.5 %all-to-all-done = bf16[32,32,256]{2,1,0:T(8,128)(2,1)S(1)} async-done(((bf16[32,32,256]{2,1,0:T(8,128)(2,1)}), bf16[32,32,256]{2,1,0:T(8,128)(2,1)S(1)}, u32[]{:S(2)}, u32[]{:S(2)}) %all-to-all-start) | async-done | bytes 524320 | tf_op jit(solution)/shard_map/while/body/eval_jaxpr/all_to_all | solution.py:29
  241.2 0.9 conditional.6
  242.9 58.1 %psum.16 = f32[32,256]{1,0:T(8,128)S(1)} all-reduce(f32[32,256]{1,0:T(8,128)S(1)} %dynamic-slice_bitcast_fusion.2), channel_id=1, replica_groups=mesh['prow'=16,'pcol'=32] {'prow'}, use_global_device_ids=true, to_apply=%region_1.1 | all-reduce | flops 8192 | bytes 65536 | tf_op jit(solution)/shard_map/while/body/eval_jaxpr/psum | solution.py:23
  302.5 18.5 %all-to-all-start = ((bf16[32,32,256]{2,1,0:T(8,128)(2,1)}), bf16[32,32,256]{2,1,0:T(8,128)(2,1)S(1)}, u32[]{:S(2)}, u32[]{:S(2)}) async-start(bf16[32,32,256]{2,1,0:T(8,128)(2,1)} %stack.8), calls=%async_computation | async-start | bytes 1048576 | tf_op jit(solution)/shard_map/while/body/eval_jaxpr/all_to_all | solution.py:29
  321.1 33.5 %all-to-all-done = bf16[32,32,256]{2,1,0:T(8,128)(2,1)S(1)} async-done(((bf16[32,32,256]{2,1,0:T(8,128)(2,1)}), bf16[32,32,256]{2,1,0:T(8,128)(2,1)S(1)}, u32[]{:S(2)}, u32[]{:S(2)}) %all-to-all-start) | async-done | bytes 524320 | tf_op jit(solution)/shard_map/while/body/eval_jaxpr/all_to_all | solution.py:29
  354.6 0.9 conditional.6
  356.3 55.6 %psum.16 = f32[32,256]{1,0:T(8,128)S(1)} all-reduce(f32[32,256]{1,0:T(8,128)S(1)} %dynamic-slice_bitcast_fusion.2), channel_id=1, replica_groups=mesh['prow'=16,'pcol'=32] {'prow'}, use_global_device_ids=true, to_apply=%region_1.1 | all-reduce | flops 8192 | bytes 65536 | tf_op jit(solution)/shard_map/while/body/eval_jaxpr/psum | solution.py:23
  413.5 18.2 %all-to-all-start = ((bf16[32,32,256]{2,1,0:T(8,128)(2,1)}), bf16[32,32,256]{2,1,0:T(8,128)(2,1)S(1)}, u32[]{:S(2)}, u32[]{:S(2)}) async-start(bf16[32,32,256]{2,1,0:T(8,128)(2,1)} %stack.8), calls=%async_computation | async-start | bytes 1048576 | tf_op jit(solution)/shard_map/while/body/eval_jaxpr/all_to_all | solution.py:29
  431.7 33.5 %all-to-all-done = bf16[32,32,256]{2,1,0:T(8,128)(2,1)S(1)} async-done(((bf16[32,32,256]{2,1,0:T(8,128)(2,1)}), bf16[32,32,256]{2,1,0:T(8,128)(2,1)S(1)}, u32[]{:S(2)}, u32[]{:S(2)}) %all-to-all-start) | async-done | bytes 524320 | tf_op jit(solution)/shard_map/while/body/eval_jaxpr/all_to_all | solution.py:29
  465.2 0.9 conditional.6
  466.9 55.6 %psum.16 = f32[32,256]{1,0:T(8,128)S(1)} all-reduce(f32[32,256]{1,0:T(8,128)S(1)} %dynamic-slice_bitcast_fusion.2), channel_id=1, replica_groups=mesh['prow'=16,'pcol'=32] {'prow'}, use_global_device_ids=true, to_apply=%region_1.1 | all-reduce | flops 8192 | bytes 65536 | tf_op jit(solution)/shard_map/while/body/eval_jaxpr/psum | solution.py:23
  524.1 18.2 %all-to-all-start = ((bf16[32,32,256]{2,1,0:T(8,128)(2,1)}), bf16[32,32,256]{2,1,0:T(8,128)(2,1)S(1)}, u32[]{:S(2)}, u32[]{:S(2)}) async-start(bf16[32,32,256]{2,1,0:T(8,128)(2,1)} %stack.8), calls=%async_computation | async-start | bytes 1048576 | tf_op jit(solution)/shard_map/while/body/eval_jaxpr/all_to_all | solution.py:29
  542.4 33.5 %all-to-all-done = bf16[32,32,256]{2,1,0:T(8,128)(2,1)S(1)} async-done(((bf16[32,32,256]{2,1,0:T(8,128)(2,1)}), bf16[32,32,256]{2,1,0:T(8,128)(2,1)S(1)}, u32[]{:S(2)}, u32[]{:S(2)}) %all-to-all-start) | async-done | bytes 524320 | tf_op jit(solution)/shard_map/while/body/eval_jaxpr/all_to_all | solution.py:29
  575.9 0.9 conditional.6
  577.5 55.6 %psum.16 = f32[32,256]{1,0:T(8,128)S(1)} all-reduce(f32[32,256]{1,0:T(8,128)S(1)} %dynamic-slice_bitcast_fusion.2), channel_id=1, replica_groups=mesh['prow'=16,'pcol'=32] {'prow'}, use_global_device_ids=true, to_apply=%region_1.1 | all-reduce | flops 8192 | bytes 65536 | tf_op jit(solution)/shard_map/while/body/eval_jaxpr/psum | solution.py:23
  634.8 18.2 %all-to-all-start = ((bf16[32,32,256]{2,1,0:T(8,128)(2,1)}), bf16[32,32,256]{2,1,0:T(8,128)(2,1)S(1)}, u32[]{:S(2)}, u32[]{:S(2)}) async-start(bf16[32,32,256]{2,1,0:T(8,128)(2,1)} %stack.8), calls=%async_computation | async-start | bytes 1048576 | tf_op jit(solution)/shard_map/while/body/eval_jaxpr/all_to_all | solution.py:29
  653.0 33.5 %all-to-all-done = bf16[32,32,256]{2,1,0:T(8,128)(2,1)S(1)} async-done(((bf16[32,32,256]{2,1,0:T(8,128)(2,1)}), bf16[32,32,256]{2,1,0:T(8,128)(2,1)S(1)}, u32[]{:S(2)}, u32[]{:S(2)}) %all-to-all-start) | async-done | bytes 524320 | tf_op jit(solution)/shard_map/while/body/eval_jaxpr/all_to_all | solution.py:29
  686.5 0.9 conditional.6
  688.2 55.6 %psum.16 = f32[32,256]{1,0:T(8,128)S(1)} all-reduce(f32[32,256]{1,0:T(8,128)S(1)} %dynamic-slice_bitcast_fusion.2), channel_id=1, replica_groups=mesh['prow'=16,'pcol'=32] {'prow'}, use_global_device_ids=true, to_apply=%region_1.1 | all-reduce | flops 8192 | bytes 65536 | tf_op jit(solution)/shard_map/while/body/eval_jaxpr/psum | solution.py:23
  745.4 18.2 %all-to-all-start = ((bf16[32,32,256]{2,1,0:T(8,128)(2,1)}), bf16[32,32,256]{2,1,0:T(8,128)(2,1)S(1)}, u32[]{:S(2)}, u32[]{:S(2)}) async-start(bf16[32,32,256]{2,1,0:T(8,128)(2,1)} %stack.8), calls=%async_computation | async-start | bytes 1048576 | tf_op jit(solution)/shard_map/while/body/eval_jaxpr/all_to_all | solution.py:29
  763.7 33.5 %all-to-all-done = bf16[32,32,256]{2,1,0:T(8,128)(2,1)S(1)} async-done(((bf16[32,32,256]{2,1,0:T(8,128)(2,1)}), bf16[32,32,256]{2,1,0:T(8,128)(2,1)S(1)}, u32[]{:S(2)}, u32[]{:S(2)}) %all-to-all-start) | async-done | bytes 524320 | tf_op jit(solution)/shard_map/while/body/eval_jaxpr/all_to_all | solution.py:29
  797.2 0.9 conditional.6
  798.8 55.6 %psum.16 = f32[32,256]{1,0:T(8,128)S(1)} all-reduce(f32[32,256]{1,0:T(8,128)S(1)} %dynamic-slice_bitcast_fusion.2), channel_id=1, replica_groups=mesh['prow'=16,'pcol'=32] {'prow'}, use_global_device_ids=true, to_apply=%region_1.1 | all-reduce | flops 8192 | bytes 65536 | tf_op jit(solution)/shard_map/while/body/eval_jaxpr/psum | solution.py:23
  856.0 18.2 %all-to-all-start = ((bf16[32,32,256]{2,1,0:T(8,128)(2,1)}), bf16[32,32,256]{2,1,0:T(8,128)(2,1)S(1)}, u32[]{:S(2)}, u32[]{:S(2)}) async-start(bf16[32,32,256]{2,1,0:T(8,128)(2,1)} %stack.8), calls=%async_computation | async-start | bytes 1048576 | tf_op jit(solution)/shard_map/while/body/eval_jaxpr/all_to_all | solution.py:29
  874.3 33.5 %all-to-all-done = bf16[32,32,256]{2,1,0:T(8,128)(2,1)S(1)} async-done(((bf16[32,32,256]{2,1,0:T(8,128)(2,1)}), bf16[32,32,256]{2,1,0:T(8,128)(2,1)S(1)}, u32[]{:S(2)}, u32[]{:S(2)}) %all-to-all-start) | async-done | bytes 524320 | tf_op jit(solution)/shard_map/while/body/eval_jaxpr/all_to_all | solution.py:29
  907.8 0.9 conditional.6
  909.5 55.6 %psum.16 = f32[32,256]{1,0:T(8,128)S(1)} all-reduce(f32[32,256]{1,0:T(8,128)S(1)} %dynamic-slice_bitcast_fusion.2), channel_id=1, replica_groups=mesh['prow'=16,'pcol'=32] {'prow'}, use_global_device_ids=true, to_apply=%region_1.1 | all-reduce | flops 8192 | bytes 65536 | tf_op jit(solution)/shard_map/while/body/eval_jaxpr/psum | solution.py:23
  966.7 18.2 %all-to-all-start = ((bf16[32,32,256]{2,1,0:T(8,128)(2,1)}), bf16[32,32,256]{2,1,0:T(8,128)(2,1)S(1)}, u32[]{:S(2)}, u32[]{:S(2)}) async-start(bf16[32,32,256]{2,1,0:T(8,128)(2,1)} %stack.8), calls=%async_computation | async-start | bytes 1048576 | tf_op jit(solution)/shard_map/while/body/eval_jaxpr/all_to_all | solution.py:29
  985.0 33.5 %all-to-all-done = bf16[32,32,256]{2,1,0:T(8,128)(2,1)S(1)} async-done(((bf16[32,32,256]{2,1,0:T(8,128)(2,1)}), bf16[32,32,256]{2,1,0:T(8,128)(2,1)S(1)}, u32[]{:S(2)}, u32[]{:S(2)}) %all-to-all-start) | async-done | bytes 524320 | tf_op jit(solution)/shard_map/while/body/eval_jaxpr/all_to_all | solution.py:29
  1020.1 55.6 %psum.16 = f32[32,256]{1,0:T(8,128)S(1)} all-reduce(f32[32,256]{1,0:T(8,128)S(1)} %dynamic-slice_bitcast_fusion.2), channel_id=1, replica_groups=mesh['prow'=16,'pcol'=32] {'prow'}, use_global_device_ids=true, to_apply=%region_1.1 | all-reduce | flops 8192 | bytes 65536 | tf_op jit(solution)/shard_map/while/body/eval_jaxpr/psum | solution.py:23
  1077.3 18.2 %all-to-all-start = ((bf16[32,32,256]{2,1,0:T(8,128)(2,1)}), bf16[32,32,256]{2,1,0:T(8,128)(2,1)S(1)}, u32[]{:S(2)}, u32[]{:S(2)}) async-start(bf16[32,32,256]{2,1,0:T(8,128)(2,1)} %stack.8), calls=%async_computation | async-start | bytes 1048576 | tf_op jit(solution)/shard_map/while/body/eval_jaxpr/all_to_all | solution.py:29
  1095.6 33.5 %all-to-all-done = bf16[32,32,256]{2,1,0:T(8,128)(2,1)S(1)} async-done(((bf16[32,32,256]{2,1,0:T(8,128)(2,1)}), bf16[32,32,256]{2,1,0:T(8,128)(2,1)S(1)}, u32[]{:S(2)}, u32[]{:S(2)}) %all-to-all-start) | async-done | bytes 524320 | tf_op jit(solution)/shard_map/while/body/eval_jaxpr/all_to_all | solution.py:29
  1130.8 55.6 %psum.16 = f32[32,256]{1,0:T(8,128)S(1)} all-reduce(f32[32,256]{1,0:T(8,128)S(1)} %dynamic-slice_bitcast_fusion.2), channel_id=1, replica_groups=mesh['prow'=16,'pcol'=32] {'prow'}, use_global_device_ids=true, to_apply=%region_1.1 | all-reduce | flops 8192 | bytes 65536 | tf_op jit(solution)/shard_map/while/body/eval_jaxpr/psum | solution.py:23
  1188.0 18.2 %all-to-all-start = ((bf16[32,32,256]{2,1,0:T(8,128)(2,1)}), bf16[32,32,256]{2,1,0:T(8,128)(2,1)S(1)}, u32[]{:S(2)}, u32[]{:S(2)}) async-start(bf16[32,32,256]{2,1,0:T(8,128)(2,1)} %stack.8), calls=%async_computation | async-start | bytes 1048576 | tf_op jit(solution)/shard_map/while/body/eval_jaxpr/all_to_all | solution.py:29
  1206.3 33.5 %all-to-all-done = bf16[32,32,256]{2,1,0:T(8,128)(2,1)S(1)} async-done(((bf16[32,32,256]{2,1,0:T(8,128)(2,1)}), bf16[32,32,256]{2,1,0:T(8,128)(2,1)S(1)}, u32[]{:S(2)}, u32[]{:S(2)}) %all-to-all-start) | async-done | bytes 524320 | tf_op jit(solution)/shard_map/while/body/eval_jaxpr/all_to_all | solution.py:29
  1239.8 0.9 conditional.6
  1241.4 55.6 %psum.16 = f32[32,256]{1,0:T(8,128)S(1)} all-reduce(f32[32,256]{1,0:T(8,128)S(1)} %dynamic-slice_bitcast_fusion.2), channel_id=1, replica_groups=mesh['prow'=16,'pcol'=32] {'prow'}, use_global_device_ids=true, to_apply=%region_1.1 | all-reduce | flops 8192 | bytes 65536 | tf_op jit(solution)/shard_map/while/body/eval_jaxpr/psum | solution.py:23
  1298.6 18.2 %all-to-all-start = ((bf16[32,32,256]{2,1,0:T(8,128)(2,1)}), bf16[32,32,256]{2,1,0:T(8,128)(2,1)S(1)}, u32[]{:S(2)}, u32[]{:S(2)}) async-start(bf16[32,32,256]{2,1,0:T(8,128)(2,1)} %stack.8), calls=%async_computation | async-start | bytes 1048576 | tf_op jit(solution)/shard_map/while/body/eval_jaxpr/all_to_all | solution.py:29
  1316.9 33.5 %all-to-all-done = bf16[32,32,256]{2,1,0:T(8,128)(2,1)S(1)} async-done(((bf16[32,32,256]{2,1,0:T(8,128)(2,1)}), bf16[32,32,256]{2,1,0:T(8,128)(2,1)S(1)}, u32[]{:S(2)}, u32[]{:S(2)}) %all-to-all-start) | async-done | bytes 524320 | tf_op jit(solution)/shard_map/while/body/eval_jaxpr/all_to_all | solution.py:29
  1352.1 55.6 %psum.16 = f32[32,256]{1,0:T(8,128)S(1)} all-reduce(f32[32,256]{1,0:T(8,128)S(1)} %dynamic-slice_bitcast_fusion.2), channel_id=1, replica_groups=mesh['prow'=16,'pcol'=32] {'prow'}, use_global_device_ids=true, to_apply=%region_1.1 | all-reduce | flops 8192 | bytes 65536 | tf_op jit(solution)/shard_map/while/body/eval_jaxpr/psum | solution.py:23
  1409.3 18.2 %all-to-all-start = ((bf16[32,32,256]{2,1,0:T(8,128)(2,1)}), bf16[32,32,256]{2,1,0:T(8,128)(2,1)S(1)}, u32[]{:S(2)}, u32[]{:S(2)}) async-start(bf16[32,32,256]{2,1,0:T(8,128)(2,1)} %stack.8), calls=%async_computation | async-start | bytes 1048576 | tf_op jit(solution)/shard_map/while/body/eval_jaxpr/all_to_all | solution.py:29
  1427.5 33.5 %all-to-all-done = bf16[32,32,256]{2,1,0:T(8,128)(2,1)S(1)} async-done(((bf16[32,32,256]{2,1,0:T(8,128)(2,1)}), bf16[32,32,256]{2,1,0:T(8,128)(2,1)S(1)}, u32[]{:S(2)}, u32[]{:S(2)}) %all-to-all-start) | async-done | bytes 524320 | tf_op jit(solution)/shard_map/while/body/eval_jaxpr/all_to_all | solution.py:29
  1461.1 0.9 conditional.6
  1462.7 55.6 %psum.16 = f32[32,256]{1,0:T(8,128)S(1)} all-reduce(f32[32,256]{1,0:T(8,128)S(1)} %dynamic-slice_bitcast_fusion.2), channel_id=1, replica_groups=mesh['prow'=16,'pcol'=32] {'prow'}, use_global_device_ids=true, to_apply=%region_1.1 | all-reduce | flops 8192 | bytes 65536 | tf_op jit(solution)/shard_map/while/body/eval_jaxpr/psum | solution.py:23
  1519.9 18.2 %all-to-all-start = ((bf16[32,32,256]{2,1,0:T(8,128)(2,1)}), bf16[32,32,256]{2,1,0:T(8,128)(2,1)S(1)}, u32[]{:S(2)}, u32[]{:S(2)}) async-start(bf16[32,32,256]{2,1,0:T(8,128)(2,1)} %stack.8), calls=%async_computation | async-start | bytes 1048576 | tf_op jit(solution)/shard_map/while/body/eval_jaxpr/all_to_all | solution.py:29
  1538.2 33.5 %all-to-all-done = bf16[32,32,256]{2,1,0:T(8,128)(2,1)S(1)} async-done(((bf16[32,32,256]{2,1,0:T(8,128)(2,1)}), bf16[32,32,256]{2,1,0:T(8,128)(2,1)S(1)}, u32[]{:S(2)}, u32[]{:S(2)}) %all-to-all-start) | async-done | bytes 524320 | tf_op jit(solution)/shard_map/while/body/eval_jaxpr/all_to_all | solution.py:29
  1573.4 55.6 %psum.16 = f32[32,256]{1,0:T(8,128)S(1)} all-reduce(f32[32,256]{1,0:T(8,128)S(1)} %dynamic-slice_bitcast_fusion.2), channel_id=1, replica_groups=mesh['prow'=16,'pcol'=32] {'prow'}, use_global_device_ids=true, to_apply=%region_1.1 | all-reduce | flops 8192 | bytes 65536 | tf_op jit(solution)/shard_map/while/body/eval_jaxpr/psum | solution.py:23
  1630.6 18.2 %all-to-all-start = ((bf16[32,32,256]{2,1,0:T(8,128)(2,1)}), bf16[32,32,256]{2,1,0:T(8,128)(2,1)S(1)}, u32[]{:S(2)}, u32[]{:S(2)}) async-start(bf16[32,32,256]{2,1,0:T(8,128)(2,1)} %stack.8), calls=%async_computation | async-start | bytes 1048576 | tf_op jit(solution)/shard_map/while/body/eval_jaxpr/all_to_all | solution.py:29
  1648.8 33.5 %all-to-all-done = bf16[32,32,256]{2,1,0:T(8,128)(2,1)S(1)} async-done(((bf16[32,32,256]{2,1,0:T(8,128)(2,1)}), bf16[32,32,256]{2,1,0:T(8,128)(2,1)S(1)}, u32[]{:S(2)}, u32[]{:S(2)}) %all-to-all-start) | async-done | bytes 524320 | tf_op jit(solution)/shard_map/while/body/eval_jaxpr/all_to_all | solution.py:29
  1682.4 0.9 conditional.6
  1684.0 55.6 %psum.16 = f32[32,256]{1,0:T(8,128)S(1)} all-reduce(f32[32,256]{1,0:T(8,128)S(1)} %dynamic-slice_bitcast_fusion.2), channel_id=1, replica_groups=mesh['prow'=16,'pcol'=32] {'prow'}, use_global_device_ids=true, to_apply=%region_1.1 | all-reduce | flops 8192 | bytes 65536 | tf_op jit(solution)/shard_map/while/body/eval_jaxpr/psum | solution.py:23
  1741.2 18.2 %all-to-all-start = ((bf16[32,32,256]{2,1,0:T(8,128)(2,1)}), bf16[32,32,256]{2,1,0:T(8,128)(2,1)S(1)}, u32[]{:S(2)}, u32[]{:S(2)}) async-start(bf16[32,32,256]{2,1,0:T(8,128)(2,1)} %stack.8), calls=%async_computation | async-start | bytes 1048576 | tf_op jit(solution)/shard_map/while/body/eval_jaxpr/all_to_all | solution.py:29
  1759.5 33.5 %all-to-all-done = bf16[32,32,256]{2,1,0:T(8,128)(2,1)S(1)} async-done(((bf16[32,32,256]{2,1,0:T(8,128)(2,1)}), bf16[32,32,256]{2,1,0:T(8,128)(2,1)S(1)}, u32[]{:S(2)}, u32[]{:S(2)}) %all-to-all-start) | async-done | bytes 524320 | tf_op jit(solution)/shard_map/while/body/eval_jaxpr/all_to_all | solution.py:29
  (150 shorter events, 54.8 us)
Async XLA Ops:
  63.2 63.3 %all-to-all-start = ((bf16[32,32,256]{2,1,0:T(8,128)(2,1)}), bf16[32,32,256]{2,1,0:T(8,128)(2,1)S(1)}, u32[]{:S(2)}, u32[]{:S(2)}) async-start(bf16[32,32,256]{2,1,0:T(8,128)(2,1)} %stack.8), calls=%async_computation | async-start | bytes 1048576 | tf_op jit(solution)/shard_map/while/body/eval_jaxpr/all_to_all | solution.py:29
  126.5 4.2 copy-start
  190.2 51.0 %all-to-all-start = ((bf16[32,32,256]{2,1,0:T(8,128)(2,1)}), bf16[32,32,256]{2,1,0:T(8,128)(2,1)S(1)}, u32[]{:S(2)}, u32[]{:S(2)}) async-start(bf16[32,32,256]{2,1,0:T(8,128)(2,1)} %stack.8), calls=%async_computation | async-start | bytes 1048576 | tf_op jit(solution)/shard_map/while/body/eval_jaxpr/all_to_all | solution.py:29
  241.2 1.4 copy-start
  302.5 52.1 %all-to-all-start = ((bf16[32,32,256]{2,1,0:T(8,128)(2,1)}), bf16[32,32,256]{2,1,0:T(8,128)(2,1)S(1)}, u32[]{:S(2)}, u32[]{:S(2)}) async-start(bf16[32,32,256]{2,1,0:T(8,128)(2,1)} %stack.8), calls=%async_computation | async-start | bytes 1048576 | tf_op jit(solution)/shard_map/while/body/eval_jaxpr/all_to_all | solution.py:29
  354.6 1.4 copy-start
  413.5 51.8 %all-to-all-start = ((bf16[32,32,256]{2,1,0:T(8,128)(2,1)}), bf16[32,32,256]{2,1,0:T(8,128)(2,1)S(1)}, u32[]{:S(2)}, u32[]{:S(2)}) async-start(bf16[32,32,256]{2,1,0:T(8,128)(2,1)} %stack.8), calls=%async_computation | async-start | bytes 1048576 | tf_op jit(solution)/shard_map/while/body/eval_jaxpr/all_to_all | solution.py:29
  465.2 1.4 copy-start
  524.1 51.8 %all-to-all-start = ((bf16[32,32,256]{2,1,0:T(8,128)(2,1)}), bf16[32,32,256]{2,1,0:T(8,128)(2,1)S(1)}, u32[]{:S(2)}, u32[]{:S(2)}) async-start(bf16[32,32,256]{2,1,0:T(8,128)(2,1)} %stack.8), calls=%async_computation | async-start | bytes 1048576 | tf_op jit(solution)/shard_map/while/body/eval_jaxpr/all_to_all | solution.py:29
  575.9 1.4 copy-start
  634.8 51.8 %all-to-all-start = ((bf16[32,32,256]{2,1,0:T(8,128)(2,1)}), bf16[32,32,256]{2,1,0:T(8,128)(2,1)S(1)}, u32[]{:S(2)}, u32[]{:S(2)}) async-start(bf16[32,32,256]{2,1,0:T(8,128)(2,1)} %stack.8), calls=%async_computation | async-start | bytes 1048576 | tf_op jit(solution)/shard_map/while/body/eval_jaxpr/all_to_all | solution.py:29
  686.5 1.4 copy-start
  745.4 51.8 %all-to-all-start = ((bf16[32,32,256]{2,1,0:T(8,128)(2,1)}), bf16[32,32,256]{2,1,0:T(8,128)(2,1)S(1)}, u32[]{:S(2)}, u32[]{:S(2)}) async-start(bf16[32,32,256]{2,1,0:T(8,128)(2,1)} %stack.8), calls=%async_computation | async-start | bytes 1048576 | tf_op jit(solution)/shard_map/while/body/eval_jaxpr/all_to_all | solution.py:29
  797.2 1.4 copy-start
  856.0 51.8 %all-to-all-start = ((bf16[32,32,256]{2,1,0:T(8,128)(2,1)}), bf16[32,32,256]{2,1,0:T(8,128)(2,1)S(1)}, u32[]{:S(2)}, u32[]{:S(2)}) async-start(bf16[32,32,256]{2,1,0:T(8,128)(2,1)} %stack.8), calls=%async_computation | async-start | bytes 1048576 | tf_op jit(solution)/shard_map/while/body/eval_jaxpr/all_to_all | solution.py:29
  907.8 1.4 copy-start
  966.7 51.8 %all-to-all-start = ((bf16[32,32,256]{2,1,0:T(8,128)(2,1)}), bf16[32,32,256]{2,1,0:T(8,128)(2,1)S(1)}, u32[]{:S(2)}, u32[]{:S(2)}) async-start(bf16[32,32,256]{2,1,0:T(8,128)(2,1)} %stack.8), calls=%async_computation | async-start | bytes 1048576 | tf_op jit(solution)/shard_map/while/body/eval_jaxpr/all_to_all | solution.py:29
  1018.5 1.4 copy-start
  1077.3 51.8 %all-to-all-start = ((bf16[32,32,256]{2,1,0:T(8,128)(2,1)}), bf16[32,32,256]{2,1,0:T(8,128)(2,1)S(1)}, u32[]{:S(2)}, u32[]{:S(2)}) async-start(bf16[32,32,256]{2,1,0:T(8,128)(2,1)} %stack.8), calls=%async_computation | async-start | bytes 1048576 | tf_op jit(solution)/shard_map/while/body/eval_jaxpr/all_to_all | solution.py:29
  1129.1 1.4 copy-start
  1188.0 51.8 %all-to-all-start = ((bf16[32,32,256]{2,1,0:T(8,128)(2,1)}), bf16[32,32,256]{2,1,0:T(8,128)(2,1)S(1)}, u32[]{:S(2)}, u32[]{:S(2)}) async-start(bf16[32,32,256]{2,1,0:T(8,128)(2,1)} %stack.8), calls=%async_computation | async-start | bytes 1048576 | tf_op jit(solution)/shard_map/while/body/eval_jaxpr/all_to_all | solution.py:29
  1239.8 1.4 copy-start
  1298.6 51.8 %all-to-all-start = ((bf16[32,32,256]{2,1,0:T(8,128)(2,1)}), bf16[32,32,256]{2,1,0:T(8,128)(2,1)S(1)}, u32[]{:S(2)}, u32[]{:S(2)}) async-start(bf16[32,32,256]{2,1,0:T(8,128)(2,1)} %stack.8), calls=%async_computation | async-start | bytes 1048576 | tf_op jit(solution)/shard_map/while/body/eval_jaxpr/all_to_all | solution.py:29
  1350.4 1.4 copy-start
  1409.3 51.8 %all-to-all-start = ((bf16[32,32,256]{2,1,0:T(8,128)(2,1)}), bf16[32,32,256]{2,1,0:T(8,128)(2,1)S(1)}, u32[]{:S(2)}, u32[]{:S(2)}) async-start(bf16[32,32,256]{2,1,0:T(8,128)(2,1)} %stack.8), calls=%async_computation | async-start | bytes 1048576 | tf_op jit(solution)/shard_map/while/body/eval_jaxpr/all_to_all | solution.py:29
  1461.1 1.4 copy-start
  1519.9 51.8 %all-to-all-start = ((bf16[32,32,256]{2,1,0:T(8,128)(2,1)}), bf16[32,32,256]{2,1,0:T(8,128)(2,1)S(1)}, u32[]{:S(2)}, u32[]{:S(2)}) async-start(bf16[32,32,256]{2,1,0:T(8,128)(2,1)} %stack.8), calls=%async_computation | async-start | bytes 1048576 | tf_op jit(solution)/shard_map/while/body/eval_jaxpr/all_to_all | solution.py:29
  1571.7 1.4 copy-start
  1630.6 51.8 %all-to-all-start = ((bf16[32,32,256]{2,1,0:T(8,128)(2,1)}), bf16[32,32,256]{2,1,0:T(8,128)(2,1)S(1)}, u32[]{:S(2)}, u32[]{:S(2)}) async-start(bf16[32,32,256]{2,1,0:T(8,128)(2,1)} %stack.8), calls=%async_computation | async-start | bytes 1048576 | tf_op jit(solution)/shard_map/while/body/eval_jaxpr/all_to_all | solution.py:29
  1682.3 1.4 copy-start
  1741.2 51.8 %all-to-all-start = ((bf16[32,32,256]{2,1,0:T(8,128)(2,1)}), bf16[32,32,256]{2,1,0:T(8,128)(2,1)S(1)}, u32[]{:S(2)}, u32[]{:S(2)}) async-start(bf16[32,32,256]{2,1,0:T(8,128)(2,1)} %stack.8), calls=%async_computation | async-start | bytes 1048576 | tf_op jit(solution)/shard_map/while/body/eval_jaxpr/all_to_all | solution.py:29
  1793.0 1.4 copy-start
  1794.6 0.8 copy-start.1
